TPU v7x, 512 devices: a whole 4x8x8 slice. The times are simulated.
512 devices in a mesh: hyp: 8 (over y), prow: 16 (over x, z_lo), pcol: 4 (over z_hi, core).
Axes of the slice: x: 4, y: 8, z: 8 (z_hi: 2, z_lo: 4; z = z_hi * 4 + z_lo), core: 2. Of those that a mesh axis runs over, the one named last changes fastest.
Arguments:
- sigma_rows: bfloat16 [8, 8192, 8192], P('hyp', 'prow', 'pcol'), may hold values from -1 to 1, as said below
- panel: bfloat16 [8, 8192, 2, 384], P('hyp', ('prow', 'pcol')), may hold values from -0.59765625 to 0.59765625
- live_block_rows: int32 [2, 64], P(None, ('prow', 'pcol')), may hold values from 1 to 128, 6144 in all within a row
- inv_diag: bfloat16 [8, 2, 384, 384], P('hyp', None, ('prow', 'pcol')), may hold values from -0.3125 to 0.3125
- quad_weight: float32 [8], P('hyp'), may hold values from 0.05 to 0.5
Outputs:
- sigma_panel: bfloat16 [8, 8192, 2, 384], P('hyp', ('prow', 'pcol'))
- marginal: float32 [2, 384, 384], replicated
Inputs may be any that keep to these rules, and one draw needn't show every extreme that they name: `sigma_rows`: each quadrature point's matrix is symmetric.
All inputs are finite; a program needn't handle non-finite values. No bound on the sum of `live_block_rows` on one device may be relied on, other than what follows from the above.
Results may differ from a plain program's by a relative error of at most 0.0004.
Values may be sent and summed in bfloat16 or wider, within the bound.
A program may use at most 64 MiB of HBM per device.

v0:
```python
import jax
import jax.numpy as jnp
from jax import lax
from jax.sharding import PartitionSpec as P


def cut_along(x, dim, length):
    shape = x.shape
    pieces = x.reshape(*shape[:dim], length, shape[dim] // length, *shape[dim + 1 :])
    return jnp.moveaxis(pieces, dim, 0)


def sent_and_summed(x, axis, dim):
    length = lax.axis_size(axis)
    pieces = lax.all_to_all(cut_along(x, dim, length), axis, 0, 0, tiled=True)
    return jnp.sum(pieces, axis=0)


def on_device(sigma_rows, panel, live_block_rows, inv_diag, quad_weight):
    height = panel.shape[1]
    width = panel.shape[3]
    supernode_list = panel.shape[2]
    offsets = lax.broadcasted_iota(jnp.int32, (height, supernode_list), 0)
    active = offsets < live_block_rows[:, 0][None, :]
    masked_panel = jnp.where(active[:, :, None], panel[0], jnp.zeros_like(panel[0]))
    grid_rows = lax.axis_size("prow")
    column = lax.axis_index("pcol")
    gathered = lax.all_gather(masked_panel, ("prow", "pcol"), axis=0, tiled=True)
    extent = height * grid_rows
    column_panel = lax.dynamic_slice_in_dim(gathered, column * extent, extent, 0)
    flattened = column_panel.reshape(column_panel.shape[0], supernode_list * width)
    covariance_block = sigma_rows[0]
    applied = sent_and_summed(
        jnp.dot(covariance_block, flattened, preferred_element_type=jnp.float32), "pcol", 0
    )
    applied_full = applied.reshape(height, supernode_list, width)
    half_applied_product = applied_full.astype(jnp.bfloat16)
    sigma_panel = jnp.where(
        active[:, :, None], -half_applied_product, jnp.zeros_like(half_applied_product)
    )[None]
    coupling_block = jnp.einsum(
        "vwg,vwe->wge",
        masked_panel.astype(jnp.float32),
        applied_full,
        precision=lax.Precision.HIGHEST,
    )
    inverse_local = inv_diag[0]
    diagonal = jnp.einsum(
        "skp,skq->spq", inverse_local, inverse_local, preferred_element_type=jnp.float32
    )
    partial_sum = coupling_block + diagonal
    marginal = lax.psum(quad_weight[0] * partial_sum, ("hyp", "prow", "pcol"))
    return (sigma_panel, marginal)


def solution(mesh):
    in_specs = (
        P("hyp", "prow", "pcol"),
        P("hyp", ("prow", "pcol"), None, None),
        P(None, ("prow", "pcol")),
        P("hyp", None, ("prow", "pcol"), None),
        P("hyp"),
    )
    out_specs = (P("hyp", ("prow", "pcol"), None, None), P())
    return jax.shard_map(
        on_device, mesh=mesh, in_specs=in_specs, out_specs=out_specs, check_vma=False
    )
```

profile of v0, /device:TPU:1, one launch (start us, length us, event | category | flops | bytes accessed | tf_op | source)
XLA Modules:
  0.0 488.1 jit_solution(7371981305845828398)
XLA Ops:
  7.2 0.0 copy-start
  7.2 0.0 all-gather.2.cloned.1.call-start
  7.2 0.8 iota_compare_fusion
  8.0 1.9 broadcast_select_fusion
  9.9 0.0 all-gather.2.cloned.1.call-update
  10.0 135.1 %all-gather.2.cloned.1.call-done = bf16[8192,2,384]{2,1,0:T(2,128)(2,1)} async-done(((bf16[128,2,384]{2,1,0:T(2,128)(2,1)}), bf16[8192,2,384]{2,1,0:T(2,128)(2,1)}) %all-gather.2.cloned.1.call-update) | async-done | bytes 12582928 | tf_op jit(solution)/shard_map/all_gather | solution.py:28
  145.1 4.7 constant_dynamic-slice_fusion
  149.8 0.6 copy.21
  150.4 2.9 fusion
  153.4 6.0 %all-to-all-start = ((f32[4,128,768]{2,1,0:T(8,128)}), f32[4,128,768]{2,1,0:T(8,128)}, u32[]{:S(2)}, u32[]{:S(2)}) async-start(f32[4,128,768]{2,1,0:T(8,128)} %bitcast.19), calls=%async_computation | async-start | bytes 3145728 | tf_op jit(solution)/shard_map/all_to_all | solution.py:15
  160.0 0.0 copy-done.2
  160.1 0.4 fusion.4
  160.4 0.0 copy-start.1
  160.4 29.1 %all-to-all-done = f32[4,128,768]{2,1,0:T(8,128)} async-done(((f32[4,128,768]{2,1,0:T(8,128)}), f32[4,128,768]{2,1,0:T(8,128)}, u32[]{:S(2)}, u32[]{:S(2)}) %all-to-all-start) | async-done | bytes 1572896 | tf_op jit(solution)/shard_map/all_to_all | solution.py:15
  189.5 2.3 reduce_sum.9
  191.8 1.9 copy.15
  193.7 0.0 copy-done.1
  193.7 2.7 fusion.2
  196.4 0.0 all-reduce.2.cloned.1.call-update
  196.4 1.0 convert_negate_fusion
  197.5 0.1 neg.14
  197.5 1.0 broadcast_select_fusion.1
  198.5 280.4 %all-reduce.2.cloned.1.call-done = f32[2,384,384]{2,1,0:T(8,128)} async-done(((f32[2,384,384]{2,1,0:T(8,128)}), f32[2,384,384]{2,1,0:T(8,128)}) %all-reduce.2.cloned.1.call-update) | async-done | bytes 1179664 | tf_op jit(solution)/shard_map/psum | solution.py:52
  478.9 2.4 copy.28
  (3 shorter events, 0.0 us)
Async XLA Ops:
  7.2 143.2 %copy-start = (bf16[1,512,2048]{2,1,0:T(8,128)(2,1)S(1)}, bf16[1,512,2048]{2,1,0:T(8,128)(2,1)}, u32[]{:S(2)}) copy-start(bf16[1,512,2048]{2,1,0:T(8,128)(2,1)} %param.5) | copy-start | bytes 6291460
  7.2 137.9 %all-gather.2.cloned.1.call-start = ((), (), s32[]{:S(2)}) async-start(), calls=%async_computation.1 | async-start | bytes 12779520 | tf_op jit(solution)/shard_map/all_gather | solution.py:28
  153.3 6.7 %copy-start.2 = (bf16[1,2,6,384]{3,1,2,0:T(2,128)(2,1)S(1)}, bf16[1,2,6,384]{3,1,2,0:T(2,128)(2,1)}, u32[]{:S(2)}) copy-start(bf16[1,2,6,384]{3,1,2,0:T(2,128)(2,1)} %param.8) | copy-start | bytes 27652
  153.4 36.2 %all-to-all-start = ((f32[4,128,768]{2,1,0:T(8,128)}), f32[4,128,768]{2,1,0:T(8,128)}, u32[]{:S(2)}, u32[]{:S(2)}) async-start(f32[4,128,768]{2,1,0:T(8,128)} %bitcast.19), calls=%async_computation | async-start | bytes 3145728 | tf_op jit(solution)/shard_map/all_to_all | solution.py:15
  159.4 319.5 %all-reduce.2.cloned.1.call-start = ((), (), s32[]{:S(2)}) async-start(), calls=%async_computation.2 | async-start | bytes 2359296 | tf_op jit(solution)/shard_map/psum | solution.py:52
  160.4 33.3 %copy-start.1 = (bf16[128,2,384]{2,1,0:T(2,128)(2,1)S(1)}, bf16[128,2,384]{2,1,0:T(2,128)(2,1)}, u32[]{:S(2)}) copy-start(bf16[128,2,384]{2,1,0:T(2,128)(2,1)} %broadcast_select_fusion) | copy-start | bytes 589828
Sparse Core Ops, SparseCore 0:
  10.7 134.2 all-gather.1
  196.6 282.2 all-reduce.1
where the time goes:
time: 489 us; the launch traced here: 488 us
  waiting for transfers between devices  445 us (91%)
  between operations  14.8 us (3%)
  local copies, waits for them, and re-layouts  9.67 us (2%)
  other arithmetic  6.99 us (1%)
  starting transfers between devices  6.08 us (1%)
  matrix products  6.01 us (1%)
    psum x1, waiting for transfers between devices, on_device(): marginal = lax.psum(quad_weight[0] * partial_sum, ('hyp', 'prow', 'pcol'))  280 us
    all_gather x1, waiting for transfers between devices, on_device(): lax.all_gather(masked_panel, ('prow', 'pcol'), axis=0, tiled=True)  135 us
    all_to_all x1, waiting for transfers between devices, sent_and_summed(): pieces = lax.all_to_all(cut_along(x, dim, length), axis, 0, 0, tiled=True)  29.1 us
  transfers between devices with their start and end apart: 3, of which 3 were waited for; matrix products, arithmetic and copies ran while one was open for 0% of the time, Pallas kernels for 0%

commit v1 on v0

--- a/solution.py
+++ b/solution.py
@@ -25,7 +25,8 @@
     masked_panel = jnp.where(active[:, :, None], panel[0], jnp.zeros_like(panel[0]))
     grid_rows = lax.axis_size("prow")
     column = lax.axis_index("pcol")
-    gathered = lax.all_gather(masked_panel, ("prow", "pcol"), axis=0, tiled=True)
+    repeated = jnp.stack([masked_panel] * lax.axis_size(("prow", "pcol")))
+    gathered = jnp.concatenate(lax.all_to_all(repeated, ("prow", "pcol"), 0, 0), axis=0)
     extent = height * grid_rows
     column_panel = lax.dynamic_slice_in_dim(gathered, column * extent, extent, 0)
     flattened = column_panel.reshape(column_panel.shape[0], supernode_list * width)

time: 489 us -> 650 us (1.33)
  waiting for transfers between devices: 445 us -> 581 us
  starting transfers between devices: 6.08 us -> 23.6 us
  local copies, waits for them, and re-layouts: 9.67 us -> 17.8 us
    all_to_all x0 -> x1, waiting for transfers between devices: none -> 273 us  [on_device(): lax.all_to_all(repeated, ('prow', 'pcol'), 0, 0)]
    all_gather x1 -> x0, waiting for transfers between devices: 135 us -> none  [on_device(): lax.all_gather(masked_panel, ('prow', 'pcol'), axis=0, tiled=True)]
    all_to_all x0 -> x1, starting transfers between devices: none -> 15 us  [on_device(): lax.all_to_all(repeated, ('prow', 'pcol'), 0, 0)]
    another operation x0 -> x1, local copies, waits for them, and re-layouts: none -> 8.13 us  [on_device(): repeated = jnp.stack([masked_panel] * lax.axis_size(('prow', 'pcol')))]
where the time goes in v1:
time: 650 us
  waiting for transfers between devices  581 us (89%)
  starting transfers between devices  23.6 us (4%)
  local copies, waits for them, and re-layouts  17.8 us (3%)
  between operations  14.8 us (2%)
  other arithmetic  6.61 us (1%)
    psum x1, waiting for transfers between devices, on_device(): marginal = lax.psum(quad_weight[0] * partial_sum, ('hyp', 'prow', 'pcol'))  280 us
    all_to_all x1, waiting for transfers between devices, on_device(): lax.all_to_all(repeated, ('prow', 'pcol'), 0, 0)  273 us
    all_to_all x1, waiting for transfers between devices, sent_and_summed(): pieces = lax.all_to_all(cut_along(x, dim, length), axis, 0, 0, tiled=True)  28 us
    all_to_all x1, starting transfers between devices, on_device(): lax.all_to_all(repeated, ('prow', 'pcol'), 0, 0)  15 us
  transfers between devices with their start and end apart: 3, of which 3 were waited for; matrix products, arithmetic and copies ran while one was open for 0% of the time, Pallas kernels for 0%

profile of v1, /device:TPU:1, one launch (start us, length us, event | category | flops | bytes accessed | tf_op | source)
XLA Modules:
  0.0 649.7 jit_solution(7444574902736371328)
XLA Ops:
  7.2 0.0 copy-start
  7.2 0.8 iota_compare_fusion
  8.0 1.2 fusion.3
  9.2 8.1 %stack.5 = bf16[64,128,2,384]{3,2,1,0:T(2,128)(2,1)} broadcast(bf16[128,2,384]{2,1,0:T(2,128)(2,1)S(1)} %fusion.3), dimensions={1,2,3} | broadcast | bytes 12779520 | tf_op jit(solution)/shard_map/stack | solution.py:28
  17.4 15.0 %all-to-all-start = ((bf16[64,128,2,384]{3,2,1,0:T(2,128)(2,1)}), bf16[64,128,2,384]{3,2,1,0:T(2,128)(2,1)}, u32[]{:S(2)}, u32[]{:S(2)}) async-start(bf16[64,128,2,384]{3,2,1,0:T(2,128)(2,1)} %stack.5), calls=%async_computation | async-start | bytes 25165824 | tf_op jit(solution)/shard_map/all_to_all | solution.py:29
  32.4 272.8 %all-to-all-done = bf16[64,128,2,384]{3,2,1,0:T(2,128)(2,1)} async-done(((bf16[64,128,2,384]{3,2,1,0:T(2,128)(2,1)}), bf16[64,128,2,384]{3,2,1,0:T(2,128)(2,1)}, u32[]{:S(2)}, u32[]{:S(2)}) %all-to-all-start) | async-done | bytes 12582944 | tf_op jit(solution)/shard_map/all_to_all | solution.py:29
  305.1 4.7 constant_dynamic-slice_fusion
  309.8 0.6 copy.21
  310.5 2.9 fusion
  313.4 8.6 %all-to-all-start.1 = ((f32[4,128,768]{2,1,0:T(8,128)}), f32[4,128,768]{2,1,0:T(8,128)}, u32[]{:S(2)}, u32[]{:S(2)}) async-start(f32[4,128,768]{2,1,0:T(8,128)} %bitcast.22), calls=%async_computation.1 | async-start | bytes 3145728 | tf_op jit(solution)/shard_map/all_to_all | solution.py:15
  322.0 0.0 all-reduce.2.cloned.1.call-start
  322.7 0.3 broadcast_select_fusion
  323.0 0.0 copy-done.2
  323.0 0.4 fusion.5
  323.4 28.0 %all-to-all-done.1 = f32[4,128,768]{2,1,0:T(8,128)} async-done(((f32[4,128,768]{2,1,0:T(8,128)}), f32[4,128,768]{2,1,0:T(8,128)}, u32[]{:S(2)}, u32[]{:S(2)}) %all-to-all-start.1) | async-done | bytes 1572896 | tf_op jit(solution)/shard_map/all_to_all | solution.py:15
  351.4 2.3 reduce_sum.9
  353.7 1.9 copy.15
  355.6 2.7 fusion.2
  358.3 0.0 all-reduce.2.cloned.1.call-update
  358.3 1.0 convert_negate_fusion
  359.3 0.1 neg.14
  359.4 1.0 broadcast_select_fusion.1
  360.4 280.1 %all-reduce.2.cloned.1.call-done = f32[2,384,384]{2,1,0:T(8,128)} async-done(((f32[2,384,384]{2,1,0:T(8,128)}), f32[2,384,384]{2,1,0:T(8,128)}) %all-reduce.2.cloned.1.call-update) | async-done | bytes 1179664 | tf_op jit(solution)/shard_map/psum | solution.py:53
  640.5 2.4 copy.28
  (4 shorter events, 0.0 us)
Async XLA Ops:
  7.2 303.3 %copy-start = (bf16[1,512,2048]{2,1,0:T(8,128)(2,1)S(1)}, bf16[1,512,2048]{2,1,0:T(8,128)(2,1)}, u32[]{:S(2)}) copy-start(bf16[1,512,2048]{2,1,0:T(8,128)(2,1)} %param.5) | copy-start | bytes 6291460
  17.4 287.8 %all-to-all-start = ((bf16[64,128,2,384]{3,2,1,0:T(2,128)(2,1)}), bf16[64,128,2,384]{3,2,1,0:T(2,128)(2,1)}, u32[]{:S(2)}, u32[]{:S(2)}) async-start(bf16[64,128,2,384]{3,2,1,0:T(2,128)(2,1)} %stack.5), calls=%async_computation | async-start | bytes 25165824 | tf_op jit(solution)/shard_map/all_to_all | solution.py:29
  313.4 9.2 %copy-start.1 = (bf16[1,128,2,384]{3,2,1,0:T(2,128)(2,1)S(1)}, bf16[1,128,2,384]{3,2,1,0:T(2,128)(2,1)}, u32[]{:S(2)}) copy-start(bf16[1,128,2,384]{3,2,1,0:T(2,128)(2,1)} %param.6) | copy-start | bytes 589828
  313.4 9.5 %copy-start.2 = (bf16[1,2,6,384]{3,1,2,0:T(2,128)(2,1)S(1)}, bf16[1,2,6,384]{3,1,2,0:T(2,128)(2,1)}, u32[]{:S(2)}) copy-start(bf16[1,2,6,384]{3,1,2,0:T(2,128)(2,1)} %param.8) | copy-start | bytes 27652
  313.4 38.0 %all-to-all-start.1 = ((f32[4,128,768]{2,1,0:T(8,128)}), f32[4,128,768]{2,1,0:T(8,128)}, u32[]{:S(2)}, u32[]{:S(2)}) async-start(f32[4,128,768]{2,1,0:T(8,128)} %bitcast.22), calls=%async_computation.1 | async-start | bytes 3145728 | tf_op jit(solution)/shard_map/all_to_all | solution.py:15
  322.0 318.5 %all-reduce.2.cloned.1.call-start = ((), (), s32[]{:S(2)}) async-start(), calls=%async_computation.2 | async-start | bytes 2359296 | tf_op jit(solution)/shard_map/psum | solution.py:53
Sparse Core Ops, SparseCore 0:
  358.4 282.0 all-reduce.1
